TPU v7x, 32 devices: a whole 2x2x4 slice. The times are simulated.
32 devices in a mesh: clip: 2 (over x), ord: 16 (over z, y, core).
Axes of the slice: x: 2, y: 2, z: 4, core: 2. Of those that a mesh axis runs over, the one named last changes fastest.
Arguments:
- reflection: bfloat16 [2, 16384, 8192], P(None, ('clip', 'ord')), parts along dimension 1, may hold values from -0.0625 to 0.0625
- incidence: bfloat16 [2, 8192, 16], replicated, may hold values from -6 to 6
- source_shift: int32 [16, 2], P('ord'), may hold values from -8 to 8
- source_weight: float32 [16], P('ord'), may hold values from 0.1 to 1
- grid_map: int32 [4096], replicated, may hold values from 0 to 4095, each once
- pupil_mask: int32 [64, 64], replicated, may hold values 0 or 1
- pupil_phase: float32 [2, 64, 64], replicated, may hold values from -3.140625 to 3.140625
- tile_order: int32 [16], replicated, may hold values from 0 to 15, each once
Outputs:
- aerial: float32 [2048, 2, 1024], P(('clip', 'ord')), parts along dimension 0
There are 2 independent parts, one for each index of `clip`. A program takes and returns all parts, laid end to end along the dimension named above; an argument that names none is the same for every part. Nothing has to cross between parts.
Inputs may be any that keep to these rules, and one draw needn't show every extreme that they name: `grid_map`: a permutation of the 4096 pupil cells. `tile_order`: a permutation of the 16 tiles.
All inputs are finite; a program needn't handle non-finite values.
Results may differ from a plain program's by a relative error of at most 0.0003.
Values may be sent and summed in bfloat16 or wider, within the bound.
A program may use at most 128 MiB of HBM per device.

v0:
```python
import math
import jax
import jax.numpy as jnp
from jax import lax
from jax.sharding import PartitionSpec as P

PIX = 1024
HIGHEST = lax.Precision.HIGHEST


def phase_table(left_ints, right_ints, period):
    turn_index = jnp.mod(left_ints[:, None] * right_ints[None, :], period).astype(jnp.float32)
    angles = turn_index * (2.0 * math.pi / period)
    return (jnp.cos(angles), jnp.sin(angles))


def band_kernel(points, period, grid_side):
    samples = 2 * grid_side
    difference = jnp.arange(1 - grid_side, grid_side, dtype=jnp.int32)
    fine_cos, fine_sin = phase_table(points, difference, period)
    coarse_cos, coarse_sin = phase_table(jnp.arange(samples, dtype=jnp.int32), difference, samples)
    joined = jnp.einsum("pm,cm->pc", fine_cos, coarse_cos, precision=HIGHEST)
    joined = joined + jnp.einsum("pm,cm->pc", fine_sin, coarse_sin, precision=HIGHEST)
    return joined / samples


def tile_lookup(row_index, tile_order, tile_rows):
    tile_number = row_index // tile_rows
    matches = tile_number[:, None] == jnp.arange(tile_order.shape[0], dtype=jnp.int32)[None, :]
    chosen = jnp.sum(jnp.where(matches, tile_order[None, :], 0), axis=1)
    return chosen * tile_rows + row_index % tile_rows


def pupil_amplitude(grid_cells, source_shift, pupil_mask, pupil_phase):
    grid_side = pupil_mask.shape[0]
    item_count = grid_cells.shape[0]
    margin = grid_side // 8
    cells_float = grid_cells.astype(jnp.float32).reshape(item_count, 2, 2, grid_side, grid_side)
    cell_real = cells_float[:, 0]
    cell_imag = cells_float[:, 1]
    open_pad = jnp.pad(pupil_mask.astype(jnp.float32), margin)
    phase_pad = jnp.pad(pupil_phase, ((0, 0), (margin, margin), (margin, margin)))

    def window(one_shift):
        row_start = margin + one_shift[0]
        col_start = margin + one_shift[1]
        opened = lax.dynamic_slice(open_pad, (row_start, col_start), (grid_side, grid_side))
        phased = lax.dynamic_slice(
            phase_pad, (jnp.zeros((), jnp.int32), row_start, col_start), (2, grid_side, grid_side)
        )
        return (opened, phased)

    opened, phased = jax.vmap(window)(source_shift)
    phase_cos = jnp.cos(phased)[:, :, None]
    phase_sin = jnp.sin(phased)[:, :, None]
    open_scale = opened[:, None, None] * (1.0 / math.sqrt(grid_side * grid_side))
    amp_real = (cell_real[:, None] * phase_cos - cell_imag[:, None] * phase_sin) * open_scale
    amp_imag = (cell_real[:, None] * phase_sin + cell_imag[:, None] * phase_cos) * open_scale
    return (amp_real, amp_imag)


def column_pass(amp_real, amp_imag, period, points):
    grid_side = amp_real.shape[-1]
    frequency = jnp.arange(grid_side, dtype=jnp.int32) - grid_side // 2
    cosine_table, sine_table = phase_table(frequency, points, period)
    rows_real = jnp.transpose(amp_real, (3, 0, 1, 2, 4)).reshape(-1, grid_side)
    rows_imag = jnp.transpose(amp_imag, (3, 0, 1, 2, 4)).reshape(-1, grid_side)
    stacked = jnp.concatenate([rows_real, rows_imag], 1)
    to_real = jnp.concatenate([cosine_table, -sine_table], 0)
    to_imag = jnp.concatenate([sine_table, cosine_table], 0)
    part_real = jnp.dot(stacked, to_real, precision=HIGHEST).reshape(grid_side, -1)
    part_imag = jnp.dot(stacked, to_imag, precision=HIGHEST).reshape(grid_side, -1)
    return jnp.concatenate([part_real, part_imag], 0)


def row_power(columns, row_points, period, weights):
    grid_side = columns.shape[0] // 2
    frequency = jnp.arange(grid_side, dtype=jnp.int32) - grid_side // 2
    cosine_table, sine_table = phase_table(row_points, frequency, period)
    row_lift = jnp.concatenate(
        [
            jnp.concatenate([cosine_table, -sine_table], 1),
            jnp.concatenate([sine_table, cosine_table], 1),
        ],
        0,
    )
    field_rows = jnp.dot(row_lift, columns, precision=HIGHEST)
    block_rows = row_points.shape[0]
    powers = (
        field_rows[:block_rows] * field_rows[:block_rows]
        + field_rows[block_rows:] * field_rows[block_rows:]
    )
    powers = powers.reshape(block_rows, weights.shape[0], 2, 2, -1)
    return jnp.einsum("bsfpx,s->bfx", powers, weights, precision=HIGHEST)


def local(
    reflection,
    incidence,
    source_shift,
    source_weight,
    grid_map,
    pupil_mask,
    pupil_phase,
    tile_order,
):
    devices = lax.axis_size("ord")
    local_rows = reflection.shape[1]
    source_count = source_shift.shape[0]
    grid_side = pupil_mask.shape[0]
    order_count = grid_side * grid_side
    pixels = PIX
    real_part = jnp.dot(reflection[0], incidence[0], preferred_element_type=jnp.float32) - jnp.dot(
        reflection[1], incidence[1], preferred_element_type=jnp.float32
    )
    imag_part = jnp.dot(reflection[0], incidence[1], preferred_element_type=jnp.float32) + jnp.dot(
        reflection[1], incidence[0], preferred_element_type=jnp.float32
    )
    fields = jnp.stack([real_part, imag_part]).astype(jnp.bfloat16)
    by_owner = fields.reshape(2, local_rows, devices, source_count)
    inverse = jnp.argsort(grid_map)
    received = lax.all_to_all(by_owner, "ord", split_axis=2, concat_axis=1, tiled=True)
    item_count = received.shape[3]
    ordered = jnp.take(received.reshape(2, 2, order_count, item_count), inverse, axis=2)
    grid_cells = jnp.transpose(ordered, (3, 0, 1, 2))
    amp_real, amp_imag = pupil_amplitude(grid_cells, source_shift, pupil_mask, pupil_phase)
    weights = source_weight / (source_count * devices)
    tile_rows = pixels // devices
    samples = 2 * grid_side
    sample_points = jnp.arange(samples, dtype=jnp.int32)
    columns = column_pass(amp_real, amp_imag, samples, sample_points)
    local_power = row_power(columns, sample_points, samples, weights)
    summed = lax.psum(local_power, "ord")
    row_index = lax.axis_index("ord") * tile_rows + jnp.arange(tile_rows, dtype=jnp.int32)
    image_rows = tile_lookup(row_index, tile_order, tile_rows)
    kernel_rows = band_kernel(image_rows, pixels, grid_side)
    kernel_cols = band_kernel(jnp.arange(pixels, dtype=jnp.int32), pixels, grid_side)
    partial_value = jnp.dot(kernel_rows, summed.reshape(samples, 2 * samples), precision=HIGHEST)
    partial_value = partial_value.reshape(tile_rows * 2, samples)
    aerial = jnp.einsum("rd,xd->rx", partial_value, kernel_cols, precision=HIGHEST).reshape(
        tile_rows, 2, pixels
    )
    return aerial


def solution(mesh):
    in_specs = (P(None, ("clip", "ord"), None), P(), P("ord", None), P("ord"), P(), P(), P(), P())
    out_specs = P(("clip", "ord"), None, None)
    return jax.shard_map(local, mesh=mesh, in_specs=in_specs, out_specs=out_specs, check_vma=False)
```

profile of v0, /device:TPU:8, one launch (start us, length us, event | category | flops | bytes accessed | tf_op | source)
XLA Modules:
  0.0 186.6 jit_solution(11292437768441231674)
XLA Ops:
  6.5 5.8 %fusion.2 = f32[512,16]{0,1:T(8,128)S(1)} fusion(bf16[2,512,8192]{2,1,0:T(8,128)(2,1)} %param.8, bf16[2,8192,16]{1,2,0:T(8,128)(2,1)} %param.9), kind=kOutput, calls=%fused_computation.3 | convolution fusion | flops 134217728 | bytes 8683520 | tf_op jit(solution)/shard_map/dot_general | solution.py:113
  12.3 6.5 %fusion = f32[512,16]{0,1:T(8,128)S(1)} fusion(bf16[2,512,8192]{2,1,0:T(8,128)(2,1)} %param.8, bf16[2,8192,16]{1,2,0:T(8,128)(2,1)} %param.9), kind=kOutput, calls=%fused_computation.1 | convolution fusion | flops 134217728 | bytes 8683520 | tf_op jit(solution)/shard_map/dot_general | solution.py:116
  18.9 2.3 %fusion.29 = bf16[1,512,16,1]{1,2,3,0:T(8,128)(2,1)S(1)} fusion(f32[512,16]{0,1:T(8,128)S(1)} %fusion.2, bf16[2,512,8192]{2,1,0:T(8,128)(2,1)S(1)} %copy-done.4, bf16[2,8192,16]{1,2,0:T(8,128)(2,1)S(1)} %copy-done.5), kind=kOutput, calls=%fused_computation.25 | convolution fusion | flops 134234112 | bytes 8699904 | tf_op jit(solution)/shard_map/dot_general | solution.py:113
  21.1 2.3 %fusion.32 = bf16[1,512,16,1]{1,2,3,0:T(8,128)(2,1)S(1)} fusion(f32[512,16]{0,1:T(8,128)S(1)} %fusion, bf16[2,512,8192]{2,1,0:T(8,128)(2,1)S(1)} %copy-done.4, bf16[2,8192,16]{1,2,0:T(8,128)(2,1)S(1)} %copy-done.5), kind=kOutput, calls=%fused_computation.26 | convolution fusion | flops 134234112 | bytes 8699904 | tf_op jit(solution)/shard_map/dot_general | solution.py:116
  23.4 0.7 copy.39
  24.1 6.3 %all-to-all-start = ((bf16[2,512,16,1]{1,0,3,2:T(2,128)(2,1)}), bf16[2,512,16,1]{1,0,3,2:T(2,128)(2,1)S(1)}, u32[]{:S(2)}, u32[]{:S(2)}) async-start(bf16[2,512,16,1]{1,0,3,2:T(2,128)(2,1)} %copy.39), calls=%async_computation | async-start | bytes 65536 | tf_op jit(solution)/shard_map/all_to_all | solution.py:122
  30.4 0.2 all-reduce.4.cloned.1.call-start
  30.6 0.6 fusion.151
  33.8 5.8 %sort.17 = (s32[4096]{0:T(1024)}, s32[4096]{0:T(1024)S(1)}) sort(s32[4096]{0:T(1024)S(1)} %copy-done.2, s32[4096]{0:T(1024)S(1)} %iota.72), dimensions={0}, to_apply=%region_1.2 | sort | flops 49152 | bytes 65536 | tf_op jit(solution)/shard_map/jit(argsort)/sort | solution.py:121
  39.6 0.2 fusion.117
  39.8 0.3 fusion.109
  40.1 0.5 fusion.86
  41.6 2.7 %fusion.39 = f32[1024,128]{1,0:T(8,128)S(1)} fusion(s32[127]{0:T(128)S(1)} %iota_add_fusion.1), kind=kOutput, calls=%fused_computation.34 | convolution fusion | flops 201801984 | bytes 524796 | tf_op jit(solution)/shard_map/pm,cm->pc/dot_general | solution.py:22
  44.3 0.6 fusion.103
  44.9 2.7 %fusion.14 = f32[1024,128,1]{1,0,2:T(8,128)S(1)} fusion(f32[1024,128]{1,0:T(8,128)S(1)} %fusion.39, s32[127]{0:T(128)S(1)} %iota_add_fusion.1), kind=kOutput, calls=%fused_computation.17 | convolution fusion | flops 202064128 | bytes 1049084 | tf_op jit(solution)/shard_map/pm,cm->pc/dot_general | solution.py:23
  47.8 4.1 %copy.41 = bf16[2,2,4096]{1,0,2:T(2,128)(2,1)} copy(bf16[2,2,4096]{2,1,0:T(2,128)(2,1)S(1)} %reshape.285) | data formatting | bytes 65536 | tf_op jit(solution)/shard_map/reshape | solution.py:124
  51.9 15.4 %gather_fusion = bf16[4096,2,2]{2,1,0:T(2,128)(2,1)S(1)} fusion(bf16[2,2,4096]{1,0,2:T(2,128)(2,1)} %copy.41, s32[4096]{0:T(1024)S(1)} %fusion.116), kind=kCustom, calls=%fused_computation | custom fusion | bytes 81920 | tf_op jit(solution)/shard_map/jit(_take)/gather | solution.py:124
  67.2 5.8 %fusion.12 = f32[1,2,2,64,64]{2,1,4,3,0:T(2,128)S(1)} fusion(bf16[1,2,2,64,64]{2,1,4,3,0:T(2,128)(2,1)S(1)} %bitcast.80, pred[64,64]{1,0:T(8,128)(4,1)S(1)} %broadcast_in_dim.32), kind=kLoop, calls=%fused_computation.14 | loop fusion | flops 32768 | bytes 102400 | tf_op jit(solution)/shard_map/convert_element_type | solution.py:38
  73.0 6.1 %fusion.150 = (f32[1,1,2,64,64]{2,1,4,3,0:T(1,128)}, f32[1,1,2,64,64]{2,1,4,3,0:T(1,128)S(1)}) fusion(f32[1,2,2,64,64]{2,1,4,3,0:T(2,128)S(1)} %fusion.12), kind=kLoop, calls=%fused_computation.173 | loop fusion | bytes 131072 | tf_op jit(solution)/shard_map/slice | solution.py:39
  79.1 2.3 %copy.42 = f32[2,64,64]{2,0,1:T(2,128)S(1)} copy(f32[2,64,64]{0,2,1:T(8,128)} %bitcast.79) | data formatting | bytes 65536 | tf_op jit(solution)/shard_map/mul | solution.py:57
  81.4 0.7 copy.44
  82.1 0.2 subtract_multiply_fusion
  82.3 0.3 fusion.72
  82.6 0.3 fusion.76
  83.0 0.6 fusion.45
  83.8 0.4 reduce_sum.19
  84.2 0.8 copy.48
  85.0 0.6 fusion.16
  85.6 91.2 %all-reduce.4.cloned.1.call-done = f32[2,128,128]{2,1,0:T(8,128)} async-done(((f32[2,128,128]{2,1,0:T(8,128)}), f32[2,128,128]{2,1,0:T(8,128)}) %all-reduce.4.cloned.1.call-update) | async-done | bytes 131088 | tf_op jit(solution)/shard_map/psum | solution.py:133
  176.8 1.2 fusion.152
  177.9 0.6 fusion.153
  178.5 1.2 copy.47
  (37 shorter events, 0.8 us)
Async XLA Ops:
  6.5 12.3 %copy-start.4 = (bf16[2,512,8192]{2,1,0:T(8,128)(2,1)S(1)}, bf16[2,512,8192]{2,1,0:T(8,128)(2,1)}, u32[]{:S(2)}) copy-start(bf16[2,512,8192]{2,1,0:T(8,128)(2,1)} %param.8) | copy-start | bytes 50331652
  6.5 12.3 %copy-start.5 = (bf16[2,8192,16]{1,2,0:T(8,128)(2,1)S(1)}, bf16[2,8192,16]{1,2,0:T(8,128)(2,1)}, u32[]{:S(2)}) copy-start(bf16[2,8192,16]{1,2,0:T(8,128)(2,1)} %param.9) | copy-start | bytes 1572868
  18.8 11.8 %copy-start.3 = (s32[1,2]{1,0:T(1,128)S(1)}, s32[1,2]{1,0:T(1,128)}, u32[]{:S(2)}) copy-start(s32[1,2]{1,0:T(1,128)} %param.10) | copy-start | bytes 28
  18.8 14.9 %copy-start.2 = (s32[4096]{0:T(1024)S(1)}, s32[4096]{0:T(1024)}, u32[]{:S(2)}) copy-start(s32[4096]{0:T(1024)} %param.12) | copy-start | bytes 49156
  18.8 21.2 %copy-start = (f32[2,64,64]{2,1,0:T(8,128)S(1)}, f32[2,64,64]{2,1,0:T(8,128)}, u32[]{:S(2)}) copy-start(f32[2,64,64]{2,1,0:T(8,128)} %param.14) | copy-start | bytes 98308
  21.1 19.6 %copy-start.1 = (s32[64,64]{1,0:T(8,128)S(1)}, s32[64,64]{1,0:T(8,128)}, u32[]{:S(2)}) copy-start(s32[64,64]{1,0:T(8,128)} %param.13) | copy-start | bytes 49156
  21.1 20.4 %copy-start.6 = (s32[16]{0:T(128)S(1)}, s32[16]{0:T(128)}, u32[]{:S(2)}) copy-start(s32[16]{0:T(128)} %param.15) | copy-start | bytes 196
  24.1 23.6 %all-to-all-start = ((bf16[2,512,16,1]{1,0,3,2:T(2,128)(2,1)}), bf16[2,512,16,1]{1,0,3,2:T(2,128)(2,1)S(1)}, u32[]{:S(2)}, u32[]{:S(2)}) async-start(bf16[2,512,16,1]{1,0,3,2:T(2,128)(2,1)} %copy.39), calls=%async_computation | async-start | bytes 65536 | tf_op jit(solution)/shard_map/all_to_all | solution.py:122
  30.4 146.4 %all-reduce.4.cloned.1.call-start = ((), (), s32[]{:S(2)}) async-start(), calls=%async_computation.1 | async-start | bytes 262144 | tf_op jit(solution)/shard_map/psum | solution.py:133
Sparse Core Ops, SparseCore 0:
  85.1 91.5 all-reduce.3
where the time goes:
time: 187 us
  waiting for transfers between devices  91.2 us (49%)
  local copies, waits for them, and re-layouts  32.8 us (18%)
  matrix products  26.4 us (14%)
  between operations  16.9 us (9%)
  other arithmetic  12.9 us (7%)
  starting transfers between devices  6.51 us (3%)
    psum x1, waiting for transfers between devices, local(): summed = lax.psum(local_power, 'ord')  91.2 us
    gather x1, local copies, waits for them, and re-layouts, local(): jnp.take(received.reshape(2, 2, order_count, item_count), inverse, axis=2)  15.4 us
    dot_general x1, matrix products, local(): jnp.dot(reflection[1], incidence[0], preferred_element_type=jnp.float32)  6.47 us
    all_to_all x1, starting transfers between devices, local(): lax.all_to_all(by_owner, 'ord', split_axis=2, concat_axis=1, tiled=True)  6.3 us
    slice x1, local copies, waits for them, and re-layouts, pupil_amplitude(): cell_real = cells_float[:, 0]  6.12 us
    dot_general x1, matrix products, local(): jnp.dot(reflection[1], incidence[1], preferred_element_type=jnp.float32)  5.79 us
    sort x1, other arithmetic, local(): inverse = jnp.argsort(grid_map)  5.77 us
    convert_element_type x1, other arithmetic, pupil_amplitude(): grid_cells.astype(jnp.float32)  5.76 us
  transfers between devices with their start and end apart: 2, of which 1 were waited for; matrix products, arithmetic and copies ran while one was open for 8% of the time, Pallas kernels for 0%

commit v1 on v0

--- a/solution.py
+++ b/solution.py
@@ -130,7 +130,8 @@
     sample_points = jnp.arange(samples, dtype=jnp.int32)
     columns = column_pass(amp_real, amp_imag, samples, sample_points)
     local_power = row_power(columns, sample_points, samples, weights)
-    summed = lax.psum(local_power, "ord")
+    shards = lax.all_gather(local_power, "ord", axis=0, tiled=False)
+    summed = shards.sum(axis=0)
     row_index = lax.axis_index("ord") * tile_rows + jnp.arange(tile_rows, dtype=jnp.int32)
     image_rows = tile_lookup(row_index, tile_order, tile_rows)
     kernel_rows = band_kernel(image_rows, pixels, grid_side)

time: 187 us -> 134 us (0.72)
  the two profiles are of different devices: /device:TPU:8 before, /device:TPU:0 now
where the time goes in v1:
time: 134 us
  waiting for transfers between devices  36 us (27%)
  local copies, waits for them, and re-layouts  31.9 us (24%)
  matrix products  25.7 us (19%)
  between operations  16.9 us (13%)
  other arithmetic  15.8 us (12%)
  starting transfers between devices  7.64 us (6%)
    all_gather x1, waiting for transfers between devices, local(): shards = lax.all_gather(local_power, 'ord', axis=0, tiled=False)  36 us
    gather x1, local copies, waits for them, and re-layouts, local(): jnp.take(received.reshape(2, 2, order_count, item_count), inverse, axis=2)  15.4 us
    all_to_all x1, starting transfers between devices, local(): lax.all_to_all(by_owner, 'ord', split_axis=2, concat_axis=1, tiled=True)  7.41 us
    dot_general x1, matrix products, local(): jnp.dot(reflection[1], incidence[0], preferred_element_type=jnp.float32)  6.47 us
    slice x1, local copies, waits for them, and re-layouts, pupil_amplitude(): cell_real = cells_float[:, 0]  6.12 us
    dot_general x1, matrix products, local(): jnp.dot(reflection[1], incidence[1], preferred_element_type=jnp.float32)  5.79 us
    sort x1, other arithmetic, local(): inverse = jnp.argsort(grid_map)  5.77 us
    convert_element_type x1, other arithmetic, pupil_amplitude(): grid_cells.astype(jnp.float32)  5.76 us
  transfers between devices with their start and end apart: 2, of which 1 were waited for; matrix products, arithmetic and copies ran while one was open for 11% of the time, Pallas kernels for 0%

profile of v1, /device:TPU:0, one launch (start us, length us, event | category | flops | bytes accessed | tf_op | source)
XLA Modules:
  0.0 133.9 jit_solution(8457137689845953082)
XLA Ops:
  6.5 5.8 %fusion.2 = f32[512,16]{0,1:T(8,128)S(1)} fusion(bf16[2,512,8192]{2,1,0:T(8,128)(2,1)} %param.8, bf16[2,8192,16]{1,2,0:T(8,128)(2,1)} %param.9), kind=kOutput, calls=%fused_computation.3 | convolution fusion | flops 134217728 | bytes 8683520 | tf_op jit(solution)/shard_map/dot_general | solution.py:113
  12.3 6.5 %fusion = f32[512,16]{0,1:T(8,128)S(1)} fusion(bf16[2,512,8192]{2,1,0:T(8,128)(2,1)} %param.8, bf16[2,8192,16]{1,2,0:T(8,128)(2,1)} %param.9), kind=kOutput, calls=%fused_computation.1 | convolution fusion | flops 134217728 | bytes 8683520 | tf_op jit(solution)/shard_map/dot_general | solution.py:116
  18.9 2.3 %fusion.29 = bf16[1,512,16,1]{1,2,3,0:T(8,128)(2,1)S(1)} fusion(f32[512,16]{0,1:T(8,128)S(1)} %fusion.2, bf16[2,512,8192]{2,1,0:T(8,128)(2,1)S(1)} %copy-done.4, bf16[2,8192,16]{1,2,0:T(8,128)(2,1)S(1)} %copy-done.5), kind=kOutput, calls=%fused_computation.25 | convolution fusion | flops 134234112 | bytes 8699904 | tf_op jit(solution)/shard_map/dot_general | solution.py:113
  21.1 2.3 %fusion.32 = bf16[1,512,16,1]{1,2,3,0:T(8,128)(2,1)S(1)} fusion(f32[512,16]{0,1:T(8,128)S(1)} %fusion, bf16[2,512,8192]{2,1,0:T(8,128)(2,1)S(1)} %copy-done.4, bf16[2,8192,16]{1,2,0:T(8,128)(2,1)S(1)} %copy-done.5), kind=kOutput, calls=%fused_computation.26 | convolution fusion | flops 134234112 | bytes 8699904 | tf_op jit(solution)/shard_map/dot_general | solution.py:116
  23.4 0.7 copy.39
  24.1 7.4 %all-to-all-start = ((bf16[2,512,16,1]{1,0,3,2:T(2,128)(2,1)}), bf16[2,512,16,1]{1,0,3,2:T(2,128)(2,1)S(1)}, u32[]{:S(2)}, u32[]{:S(2)}) async-start(bf16[2,512,16,1]{1,0,3,2:T(2,128)(2,1)} %copy.39), calls=%async_computation | async-start | bytes 65536 | tf_op jit(solution)/shard_map/all_to_all | solution.py:122
  31.5 0.2 all-gather.3.cloned.1.call-start
  31.7 0.6 fusion.151
  34.9 5.8 %sort.17 = (s32[4096]{0:T(1024)}, s32[4096]{0:T(1024)S(1)}) sort(s32[4096]{0:T(1024)S(1)} %copy-done.2, s32[4096]{0:T(1024)S(1)} %iota.72), dimensions={0}, to_apply=%region_1.2 | sort | flops 49152 | bytes 65536 | tf_op jit(solution)/shard_map/jit(argsort)/sort | solution.py:121
  40.7 0.2 fusion.117
  40.9 0.3 fusion.109
  41.2 0.5 fusion.86
  42.7 3.9 %copy.41 = bf16[2,2,4096]{1,0,2:T(2,128)(2,1)} copy(bf16[2,2,4096]{2,1,0:T(2,128)(2,1)S(1)} %reshape.285) | data formatting | bytes 65536 | tf_op jit(solution)/shard_map/reshape | solution.py:124
  46.6 15.4 %gather_fusion = bf16[4096,2,2]{2,1,0:T(2,128)(2,1)S(1)} fusion(bf16[2,2,4096]{1,0,2:T(2,128)(2,1)} %copy.41, s32[4096]{0:T(1024)S(1)} %fusion.116), kind=kCustom, calls=%fused_computation | custom fusion | bytes 81920 | tf_op jit(solution)/shard_map/jit(_take)/gather | solution.py:124
  62.0 5.8 %fusion.12 = f32[1,2,2,64,64]{2,1,4,3,0:T(2,128)S(1)} fusion(bf16[1,2,2,64,64]{2,1,4,3,0:T(2,128)(2,1)S(1)} %bitcast.84, pred[64,64]{1,0:T(8,128)(4,1)S(1)} %broadcast_in_dim.32), kind=kLoop, calls=%fused_computation.14 | loop fusion | flops 32768 | bytes 102400 | tf_op jit(solution)/shard_map/convert_element_type | solution.py:38
  67.8 6.1 %fusion.150 = (f32[1,1,2,64,64]{2,1,4,3,0:T(1,128)}, f32[1,1,2,64,64]{2,1,4,3,0:T(1,128)S(1)}) fusion(f32[1,2,2,64,64]{2,1,4,3,0:T(2,128)S(1)} %fusion.12), kind=kLoop, calls=%fused_computation.174 | loop fusion | bytes 131072 | tf_op jit(solution)/shard_map/slice | solution.py:39
  73.9 2.3 %copy.42 = f32[2,64,64]{2,0,1:T(2,128)S(1)} copy(f32[2,64,64]{0,2,1:T(8,128)} %bitcast.83) | data formatting | bytes 65536 | tf_op jit(solution)/shard_map/mul | solution.py:57
  76.2 0.7 copy.44
  77.1 0.3 fusion.72
  77.4 0.3 fusion.76
  77.8 0.6 fusion.45
  78.6 0.4 reduce_sum.28
  79.0 0.7 broadcast_multiply_fusion
  79.8 0.6 fusion.103
  80.4 0.6 fusion.16
  81.0 2.7 %fusion.39 = f32[1024,128]{1,0:T(8,128)S(1)} fusion(s32[127]{0:T(128)S(1)} %iota_add_fusion.1), kind=kOutput, calls=%fused_computation.34 | convolution fusion | flops 201801984 | bytes 524796 | tf_op jit(solution)/shard_map/pm,cm->pc/dot_general | solution.py:22
  83.7 2.9 %fusion.14 = f32[1024,128,1]{1,0,2:T(8,128)S(1)} fusion(f32[1024,128]{1,0:T(8,128)S(1)} %fusion.39, s32[127]{0:T(128)S(1)} %iota_add_fusion.1), kind=kOutput, calls=%fused_computation.17 | convolution fusion | flops 202064128 | bytes 1049084 | tf_op jit(solution)/shard_map/pm,cm->pc/dot_general | solution.py:23
  86.6 36.0 %all-gather.3.cloned.1.call-done = f32[2048,2,128]{2,1,0:T(2,128)} async-done(((f32[128,2,128]{2,1,0:T(2,128)}), f32[2048,2,128]{2,1,0:T(2,128)}) %all-gather.3.cloned.1.call-update) | async-done | bytes 2097168 | tf_op jit(solution)/shard_map/all_gather | solution.py:133
  122.6 2.3 %reduce_sum.29 = f32[128,2,128]{2,1,0:T(2,128)S(1)} reduce(f32[16,128,2,128]{3,2,1,0:T(2,128)} %bitcast.85, f32[]{:T(128)} %constant.136.clone.1), dimensions={0}, to_apply=%region_3.4 | reduce | flops 491520 | bytes 2228228 | tf_op jit(solution)/shard_map/reduce_sum | solution.py:134
  125.0 0.3 fusion.152
  125.3 0.6 fusion.153
  125.9 1.2 copy.47
  (39 shorter events, 1.1 us)
Async XLA Ops:
  6.5 12.3 %copy-start.4 = (bf16[2,512,8192]{2,1,0:T(8,128)(2,1)S(1)}, bf16[2,512,8192]{2,1,0:T(8,128)(2,1)}, u32[]{:S(2)}) copy-start(bf16[2,512,8192]{2,1,0:T(8,128)(2,1)} %param.8) | copy-start | bytes 50331652
  6.5 12.3 %copy-start.5 = (bf16[2,8192,16]{1,2,0:T(8,128)(2,1)S(1)}, bf16[2,8192,16]{1,2,0:T(8,128)(2,1)}, u32[]{:S(2)}) copy-start(bf16[2,8192,16]{1,2,0:T(8,128)(2,1)} %param.9) | copy-start | bytes 1572868
  18.8 12.9 %copy-start.3 = (s32[1,2]{1,0:T(1,128)S(1)}, s32[1,2]{1,0:T(1,128)}, u32[]{:S(2)}) copy-start(s32[1,2]{1,0:T(1,128)} %param.10) | copy-start | bytes 28
  18.8 16.0 %copy-start.2 = (s32[4096]{0:T(1024)S(1)}, s32[4096]{0:T(1024)}, u32[]{:S(2)}) copy-start(s32[4096]{0:T(1024)} %param.12) | copy-start | bytes 49156
  18.8 22.4 %copy-start = (f32[2,64,64]{2,1,0:T(8,128)S(1)}, f32[2,64,64]{2,1,0:T(8,128)}, u32[]{:S(2)}) copy-start(f32[2,64,64]{2,1,0:T(8,128)} %param.14) | copy-start | bytes 98308
  21.1 20.7 %copy-start.1 = (s32[64,64]{1,0:T(8,128)S(1)}, s32[64,64]{1,0:T(8,128)}, u32[]{:S(2)}) copy-start(s32[64,64]{1,0:T(8,128)} %param.13) | copy-start | bytes 49156
  24.1 18.6 %all-to-all-start = ((bf16[2,512,16,1]{1,0,3,2:T(2,128)(2,1)}), bf16[2,512,16,1]{1,0,3,2:T(2,128)(2,1)S(1)}, u32[]{:S(2)}, u32[]{:S(2)}) async-start(bf16[2,512,16,1]{1,0,3,2:T(2,128)(2,1)} %copy.39), calls=%async_computation | async-start | bytes 65536 | tf_op jit(solution)/shard_map/all_to_all | solution.py:122
  31.5 91.1 %all-gather.3.cloned.1.call-start = ((), (), s32[]{:S(2)}) async-start(), calls=%async_computation.1 | async-start | bytes 2228224 | tf_op jit(solution)/shard_map/all_gather | solution.py:133
  67.8 12.0 %copy-start.6 = (s32[16]{0:T(128)S(1)}, s32[16]{0:T(128)}, u32[]{:S(2)}) copy-start(s32[16]{0:T(128)} %param.15) | copy-start | bytes 196
Sparse Core Ops, SparseCore 0:
  79.8 42.7 all-gather.2
